TPU v7x, 32 devices: a whole 2x2x4 slice. The times are simulated.
32 devices in a mesh: pipe: 2 (over core), ctx: 16 (over z, y, x).
Axes of the slice: x: 2, y: 2, z: 4, core: 2. Of those that a mesh axis runs over, the one named last changes fastest.
Arguments:
- states: bfloat16 [2, 2048, 2048], P('pipe', 'ctx'), may hold values from -6 to 6
- norm_gain: float32 [2, 2048], P('pipe'), may hold values from 0.25 to 1.75
- w_in: bfloat16 [2, 2048, 1536], P('pipe', 'ctx'), may hold values from -1 to 1
- w_out: bfloat16 [2, 1024, 2048], P('pipe', 'ctx'), may hold values from -0.1875 to 0.1875
- lengths: int32 [2, 4], replicated, may hold values from 1 to 1024, 2048 in all within a row
Outputs:
- moved: bfloat16 [2, 2048, 2048], P('pipe', 'ctx')
Inputs may be any that keep to these rules, and one draw needn't show every extreme that they name: Each row of lengths lays the responses of one micro-batch end to end over the 2048 positions.
All inputs are finite; a program needn't handle non-finite values.
Results may differ from a plain program's by a relative error of at most 0.0045.
Values may be sent and summed in bfloat16 or wider, within the bound.
No kernel may reach another device: no remote copies, remote signals or barrier semaphores. Data moves between devices by JAX's collectives and lax.ppermute only.
A program may use at most 64 MiB of HBM per device.

v0:
```python
import jax
import jax.numpy as jnp
from jax import lax
from jax.sharding import PartitionSpec as P

HEAD_DIM = 64
HEADS = 16
KV_HEADS = 4
epsilon = 1e-05
rope_base = 500000.0
masked_score = -1e30


def passed_along(value, axis, steps):
    count = lax.axis_size(axis)
    initial, last = (max(0, -steps), min(count, count - steps))
    return lax.ppermute(value, axis, [(source, source + steps) for source in range(initial, last)])


def passed_along_2(value, axis, steps):
    count = lax.axis_size(axis)
    pairs = [(source, (source + steps) % count) for source in range(count)]
    return lax.ppermute(value, axis, pairs)


def locate(doc_lengths, spots):
    doc_ends = jnp.cumsum(doc_lengths)
    segment = jnp.sum((doc_ends[None, :] <= spots[:, None]).astype(jnp.int32), axis=1)
    starts = doc_ends - doc_lengths
    labels = jnp.arange(doc_lengths.shape[0], dtype=jnp.int32)
    first = jnp.sum(jnp.where(segment[:, None] == labels[None, :], starts[None, :], 0), axis=1)
    return (segment, spots - first)


def rotate_pairs(heads_data, position):
    half_dim = heads_data.shape[-1] // 2
    inverse = rope_base ** (-jnp.arange(half_dim, dtype=jnp.float32) * 2.0 / heads_data.shape[-1])
    angles = position.astype(jnp.float32)[:, None] * inverse[None, :]
    cosine = jnp.cos(angles)[:, None, :]
    sine_part = jnp.sin(angles)[:, None, :]
    first_half = heads_data[..., :half_dim]
    second_half = heads_data[..., half_dim:]
    return jnp.concatenate(
        [
            first_half * cosine - second_half * sine_part,
            second_half * cosine + first_half * sine_part,
        ],
        -1,
    )


def body(states, norm_gain, w_in, w_out, lengths):
    section_index = lax.axis_index("pipe")
    ctx_index = lax.axis_index("ctx")
    ctx_count = lax.axis_size("ctx")
    tok_rows = states.shape[1]
    doc_lengths = lax.dynamic_index_in_dim(lengths, section_index, 0, keepdims=False)
    gain = norm_gain[0]
    weight_in = w_in[0]
    weight_out = w_out[0]
    wide = states[0].astype(jnp.float32)
    normed = (wide * lax.rsqrt(jnp.mean(wide * wide, -1, keepdims=True) + epsilon) * gain).astype(
        jnp.bfloat16
    )
    columns = normed
    proj = jnp.dot(
        columns,
        lax.all_gather(weight_in, "ctx", axis=0, tiled=True),
        preferred_element_type=jnp.float32,
    )
    q_width = HEADS * HEAD_DIM
    k_width = KV_HEADS * HEAD_DIM
    group = HEADS // KV_HEADS
    first_spot = ctx_index * tok_rows
    query_spots = first_spot + jnp.arange(tok_rows, dtype=jnp.int32)
    query_seg, position = locate(doc_lengths, query_spots)
    queries = rotate_pairs(proj[:, :q_width].reshape(tok_rows, HEADS, HEAD_DIM), position).astype(
        jnp.bfloat16
    )
    queries = queries.reshape(tok_rows, KV_HEADS, group, HEAD_DIM)
    keys_rot = rotate_pairs(
        proj[:, q_width : q_width + k_width].reshape(tok_rows, KV_HEADS, HEAD_DIM), position
    ).astype(jnp.bfloat16)
    values = proj[:, q_width + k_width :].astype(jnp.bfloat16)
    key_values = jnp.concatenate([keys_rot.reshape(tok_rows, k_width), values], 1)

    def attend_block(carry, portion, offset):
        row_count = portion.shape[0]
        key_spots = offset + jnp.arange(row_count, dtype=jnp.int32)
        key_seg, unused_place = locate(doc_lengths, key_spots)
        allowed = (
            (query_seg[:, None] == key_seg[None, :])
            & (key_spots[None, :] <= query_spots[:, None])
            & (key_spots[None, :] >= 0)
        )

        def update(state):
            running_max, running_sum, accum = state
            key_part = portion[:, :k_width].reshape(row_count, KV_HEADS, HEAD_DIM)
            value_part = portion[:, k_width:].reshape(row_count, KV_HEADS, HEAD_DIM)
            scores = jnp.einsum(
                "tgjd,rgd->gjtr", queries, key_part, preferred_element_type=jnp.float32
            ) * HEAD_DIM ** (-0.5)
            scores = jnp.where(allowed, scores, masked_score)
            new_max = jnp.maximum(running_max, jnp.max(scores, -1))
            rescale = jnp.exp(running_max - new_max)
            probs = jnp.where(allowed, jnp.exp(scores - new_max[..., None]), 0.0)
            new_sum = running_sum * rescale + jnp.sum(probs, -1)
            product = jnp.einsum(
                "gjtr,rgd->gjtd",
                probs.astype(jnp.bfloat16),
                value_part,
                preferred_element_type=jnp.float32,
            )
            return (new_max, new_sum, accum * rescale[..., None] + product)

        return lax.cond(jnp.any(allowed), update, lambda state: state, carry)

    initial = (
        jnp.full((KV_HEADS, group, tok_rows), masked_score, jnp.float32),
        jnp.zeros((KV_HEADS, group, tok_rows), jnp.float32),
        jnp.zeros((KV_HEADS, group, tok_rows, HEAD_DIM), jnp.float32),
    )
    resp_longest = min(1024, 8 * tok_rows, tok_rows * ctx_count // 2)
    reach_count = min(ctx_count - 1, (resp_longest + tok_rows - 2) // tok_rows)
    needed = reach_count + 1
    collected = key_values
    held = 1
    while held < needed:
        taken = min(held, needed - held)
        arrived = passed_along(collected[collected.shape[0] - taken * tok_rows :], "ctx", held)
        collected = jnp.concatenate([arrived, collected], 0)
        held = held + taken
    carry = initial
    portion = collected
    offset = first_spot - (held - 1) * tok_rows
    row_count = portion.shape[0]
    block_rows = min(row_count, 512)
    full_blocks = row_count // block_rows

    def visit_block(block_idx, state):
        sliced = lax.dynamic_slice_in_dim(portion, block_idx * block_rows, block_rows, 0)
        return attend_block(state, sliced, offset + block_idx * block_rows)

    carry = lax.fori_loop(0, full_blocks, visit_block, carry)
    carry = attend_block(
        carry, portion[full_blocks * block_rows :], offset + full_blocks * block_rows
    )
    running_max, running_sum, accum = carry
    attended = (
        (accum / running_sum[..., None])
        .transpose(2, 0, 1, 3)
        .reshape(tok_rows, q_width)
        .astype(jnp.bfloat16)
    )
    columns = attended
    output = jnp.dot(
        columns,
        lax.all_gather(weight_out, "ctx", axis=0, tiled=True),
        preferred_element_type=jnp.float32,
    )
    new_state = (wide + output).astype(jnp.bfloat16)
    passed = passed_along_2(new_state, "pipe", 1)
    return passed[None]


def solution(mesh):
    return jax.shard_map(
        body,
        mesh=mesh,
        in_specs=(
            P("pipe", "ctx", None),
            P("pipe", None),
            P("pipe", "ctx", None),
            P("pipe", "ctx", None),
            P(),
        ),
        out_specs=P("pipe", "ctx", None),
        check_vma=False,
    )
```

profile of v0, /device:TPU:0, one launch (start us, length us, event | category | flops | bytes accessed | tf_op | source)
XLA Modules:
  0.0 203.2 jit_solution(16966979567751797768)
XLA Ops:
  6.5 0.7 all-gather.5.cloned.1.call-update
  9.8 1.2 fusion.34
  11.1 95.1 %all-gather.5.cloned.1.call-done = bf16[1,2048,1536]{2,1,0:T(8,128)(2,1)} async-done(((bf16[1,128,1536]{2,1,0:T(8,128)(2,1)}), bf16[1,2048,1536]{2,1,0:T(8,128)(2,1)}) %all-gather.5.cloned.1.call-update) | async-done | bytes 6291472 | tf_op jit(solution)/shard_map/all_gather | solution.py:68
  106.3 4.0 %fusion.24 = f32[128,1536]{1,0:T(8,128)S(1)} fusion(bf16[1,2048,1536]{2,1,0:T(8,128)(2,1)} %all-gather.5.cloned.1.call-done, bf16[1,128,2048]{2,1,0:T(8,128)(2,1)} %param.11, f32[2048]{0:T(1024)} %bitcast.120, f32[128]{0:T(128)S(1)} %add_rsqrt_fusion), kind=kOutput, calls=%fused_computation.34 | convolution fusion | flops 806354944 | bytes 7610880 | tf_op jit(solution)/shard_map/dot_general | solution.py:66
  111.2 3.4 %collective-permute-start.1 = (bf16[128,512]{1,0:T(8,128)(2,1)}, bf16[128,512]{1,0:T(8,128)(2,1)S(1)}, u32[]{:S(2)}, u32[]{:S(2)}) collective-permute-start(bf16[128,512]{1,0:T(8,128)(2,1)} %pad_maximum_fusion.1), channel_id=1, source_target_pairs={{0,1},{1,2},{2,3},{3,4},{4,5},{5,6},{6,7},{7,8},{8,9},{9,10},{10,1... | collective-permute-start | bytes 393224 | tf_op jit(solution)/shard_map/ppermute | solution.py:17
  114.6 4.0 %collective-permute-done.1 = bf16[128,512]{1,0:T(8,128)(2,1)S(1)} collective-permute-done((bf16[128,512]{1,0:T(8,128)(2,1)}, bf16[128,512]{1,0:T(8,128)(2,1)S(1)}, u32[]{:S(2)}, u32[]{:S(2)}) %collective-permute-start.1) | collective-permute-done | bytes 131104 | tf_op jit(solution)/shard_map/ppermute | solution.py:17
  118.6 4.8 %collective-permute-start.2 = (bf16[256,512]{1,0:T(8,128)(2,1)S(1)}, bf16[256,512]{1,0:T(8,128)(2,1)S(1)}, u32[]{:S(2)}, u32[]{:S(2)}) collective-permute-start(bf16[256,512]{1,0:T(8,128)(2,1)S(1)} %maximum_maximum_fusion.1), channel_id=1, source_target_pairs={{0,2},{1,3},{2,4},{3,5},{4,6},{5,7},{6,8},{7,9},{8,10},{9,11},{10,... | collective-permute-start | bytes 786440 | tf_op jit(solution)/shard_map/ppermute | solution.py:17
  123.4 1.4 and_and_fusion.1
  124.9 2.4 %collective-permute-done.2 = bf16[256,512]{1,0:T(8,128)(2,1)S(1)} collective-permute-done((bf16[256,512]{1,0:T(8,128)(2,1)S(1)}, bf16[256,512]{1,0:T(8,128)(2,1)S(1)}, u32[]{:S(2)}, u32[]{:S(2)}) %collective-permute-start.2) | collective-permute-done | bytes 262176 | tf_op jit(solution)/shard_map/ppermute | solution.py:17
  127.3 7.6 %collective-permute-start.3 = (bf16[512,512]{1,0:T(8,128)(2,1)S(1)}, bf16[512,512]{1,0:T(8,128)(2,1)S(1)}, u32[]{:S(2)}, u32[]{:S(2)}) collective-permute-start(bf16[512,512]{1,0:T(8,128)(2,1)S(1)} %maximum_maximum_fusion), channel_id=1, source_target_pairs={{0,4},{1,5},{2,6},{3,7},{4,8},{5,9},{6,10},{7,11},{8,12},{9,13},{1... | collective-permute-start | bytes 1572872 | tf_op jit(solution)/shard_map/ppermute | solution.py:17
  135.9 5.3 %collective-permute-start = (bf16[128,512]{1,0:T(8,128)(2,1)}, bf16[128,512]{1,0:T(8,128)(2,1)}, u32[]{:S(2)}, u32[]{:S(2)}) collective-permute-start(bf16[128,512]{1,0:T(8,128)(2,1)} %pad_maximum_fusion.1), channel_id=1, source_target_pairs={{0,8},{1,9},{2,10},{3,11},{4,12},{5,13},{6,14},{7,15},{16,24},{17,... | collective-permute-start | bytes 393224 | tf_op jit(solution)/shard_map/ppermute | solution.py:17
  141.5 16.9 %collective-permute-done = bf16[128,512]{1,0:T(8,128)(2,1)} collective-permute-done((bf16[128,512]{1,0:T(8,128)(2,1)}, bf16[128,512]{1,0:T(8,128)(2,1)}, u32[]{:S(2)}, u32[]{:S(2)}) %collective-permute-start) | collective-permute-done | bytes 131104 | tf_op jit(solution)/shard_map/ppermute | solution.py:17
  158.3 1.5 constant_dynamic-update-slice_fusion.4
  159.9 0.8 constant_dynamic-update-slice_fusion.3
  160.7 0.7 constant_dynamic-update-slice_fusion.2
  162.7 1.7 copy.29
  164.5 3.7 %while.20 = (s32[]{:T(128)}, f32[4,4,128]{2,1,0:T(4,128)S(1)}, f32[4,4,128]{2,1,0:T(4,128)S(1)}, f32[4,4,128,64]{2,3,1,0:T(8,128)S(1)}, s32[128]{0:T(128)S(1)}, ...) while((s32[]{:T(128)}, f32[4,4,128]{2,1,0:T(4,128)S(1)}, ...), condition=%wide.region_13.14_spmd.clone, body=%wide.region_6.13_spmd.clone.sunk | while | flops 282668160 | bytes 15872853 | solution.py:145
  164.6 1.0 fusion.54
  166.5 1.0 fusion.54
  168.2 1.1 conditional.2
  169.4 21.3 %all-gather.7.cloned.1.call-done = bf16[1,1024,2048]{2,1,0:T(8,128)(2,1)} async-done(((bf16[1,64,2048]{2,1,0:T(8,128)(2,1)}), bf16[1,1024,2048]{2,1,0:T(8,128)(2,1)}) %all-gather.7.cloned.1.call-update) | async-done | bytes 4194320 | tf_op jit(solution)/shard_map/all_gather | solution.py:159
  190.7 2.9 %fusion.31 = bf16[128,2048]{1,0:T(8,128)(2,1)S(1)} fusion(bf16[128,1024]{0,1:T(8,128)(2,1)S(1)} %bitcast.103, bf16[1,1024,2048]{2,1,0:T(8,128)(2,1)} %all-gather.7.cloned.1.call-done, bf16[1,128,2048]{2,1,0:T(8,128)(2,1)S(1)} %copy-done), kind=kOutput, calls=%fused_computation.39 | convolution fusion | flops 537657344 | bytes 5505024 | tf_op jit(solution)/shard_map/dot_general | solution.py:157
  193.7 1.9 collective-permute-done.4
  195.6 0.8 copy.66
  (59 shorter events, 6.9 us)
Async XLA Ops:
  6.5 99.7 %all-gather.5.cloned.1.call-start = ((), (), s32[]{:S(2)}) async-start(), calls=%async_computation | async-start | bytes 6684672 | tf_op jit(solution)/shard_map/all_gather | solution.py:68
  7.3 183.4 %all-gather.7.cloned.1.call-start = ((), (), s32[]{:S(2)}) async-start(), calls=%async_computation.1 | async-start | bytes 4456448 | tf_op jit(solution)/shard_map/all_gather | solution.py:159
  106.3 28.7 %copy-start.2 = (s32[2,4]{1,0:T(2,128)S(1)}, s32[2,4]{1,0:T(2,128)}, u32[]{:S(2)}) copy-start(s32[2,4]{1,0:T(2,128)} %param.15) | copy-start | bytes 100
  111.2 7.4 %collective-permute-start.1 = (bf16[128,512]{1,0:T(8,128)(2,1)}, bf16[128,512]{1,0:T(8,128)(2,1)S(1)}, u32[]{:S(2)}, u32[]{:S(2)}) collective-permute-start(bf16[128,512]{1,0:T(8,128)(2,1)} %pad_maximum_fusion.1), channel_id=1, source_target_pairs={{0,1},{1,2},{2,3},{3,4},{4,5},{5,6},{6,7},{7,8},{8,9},{9,10},{10,1... | collective-permute-start | bytes 393224 | tf_op jit(solution)/shard_map/ppermute | solution.py:17
  118.6 8.6 %collective-permute-start.2 = (bf16[256,512]{1,0:T(8,128)(2,1)S(1)}, bf16[256,512]{1,0:T(8,128)(2,1)S(1)}, u32[]{:S(2)}, u32[]{:S(2)}) collective-permute-start(bf16[256,512]{1,0:T(8,128)(2,1)S(1)} %maximum_maximum_fusion.1), channel_id=1, source_target_pairs={{0,2},{1,3},{2,4},{3,5},{4,6},{5,7},{6,8},{7,9},{8,10},{9,11},{10,... | collective-permute-start | bytes 786440 | tf_op jit(solution)/shard_map/ppermute | solution.py:17
  127.3 32.5 %collective-permute-start.3 = (bf16[512,512]{1,0:T(8,128)(2,1)S(1)}, bf16[512,512]{1,0:T(8,128)(2,1)S(1)}, u32[]{:S(2)}, u32[]{:S(2)}) collective-permute-start(bf16[512,512]{1,0:T(8,128)(2,1)S(1)} %maximum_maximum_fusion), channel_id=1, source_target_pairs={{0,4},{1,5},{2,6},{3,7},{4,8},{5,9},{6,10},{7,11},{8,12},{9,13},{1... | collective-permute-start | bytes 1572872 | tf_op jit(solution)/shard_map/ppermute | solution.py:17
  135.9 22.5 %collective-permute-start = (bf16[128,512]{1,0:T(8,128)(2,1)}, bf16[128,512]{1,0:T(8,128)(2,1)}, u32[]{:S(2)}, u32[]{:S(2)}) collective-permute-start(bf16[128,512]{1,0:T(8,128)(2,1)} %pad_maximum_fusion.1), channel_id=1, source_target_pairs={{0,8},{1,9},{2,10},{3,11},{4,12},{5,13},{6,14},{7,15},{16,24},{17,... | collective-permute-start | bytes 393224 | tf_op jit(solution)/shard_map/ppermute | solution.py:17
  164.5 3.7 %copy-start.1 = (pred[128,128]{0,1:T(8,128)(4,1)S(1)}, pred[128,128]{0,1:T(8,128)(4,1)}, u32[]{:S(2)}) copy-start(pred[128,128]{0,1:T(8,128)(4,1)} %get-tuple-element.457) | copy-start | bytes 49156
  168.2 22.5 %copy-start = (bf16[1,128,2048]{2,1,0:T(8,128)(2,1)S(1)}, bf16[1,128,2048]{2,1,0:T(8,128)(2,1)}, u32[]{:S(2)}) copy-start(bf16[1,128,2048]{2,1,0:T(8,128)(2,1)} %param.11) | copy-start | bytes 1572868
  193.6 2.0 collective-permute-start.4
Sparse Core Ops, SparseCore 0:
  10.1 96.0 all-gather.4
  109.0 81.5 all-gather.6
where the time goes:
time: 204 us; the launch traced here: 203 us
  waiting for transfers between devices  143 us (70%)
  starting transfers between devices  21.1 us (10%)
  between operations  14.4 us (7%)
  other arithmetic  7.99 us (4%)
  matrix products  7.68 us (4%)
  local copies, waits for them, and re-layouts  7.55 us (4%)
    all_gather x1, waiting for transfers between devices, body(): lax.all_gather(weight_in, 'ctx', axis=0, tiled=True)  95.1 us
    ppermute x4, waiting for transfers between devices, passed_along(): lax.ppermute(value, axis, [(source, source + steps) for source in range(i...  23.3 us
    all_gather x1, waiting for transfers between devices, body(): lax.all_gather(weight_out, 'ctx', axis=0, tiled=True)  21.3 us
    ppermute x4, starting transfers between devices, passed_along(): lax.ppermute(value, axis, [(source, source + steps) for source in range(i...  21 us
    unnamed x12, local copies, waits for them, and re-layouts  6.25 us
  transfers between devices with their start and end apart: 7, of which 6 were waited for; matrix products, arithmetic and copies ran while one was open for 10% of the time, Pallas kernels for 0%

commit v1 on v0

--- a/solution.py
+++ b/solution.py
@@ -65,7 +65,15 @@
     columns = normed
     proj = jnp.dot(
         columns,
-        lax.all_gather(weight_in, "ctx", axis=0, tiled=True),
+        jnp.concatenate(
+            lax.all_to_all(
+                jnp.stack([weight_in] * lax.axis_size("ctx")),
+                axis_name="ctx",
+                split_axis=0,
+                concat_axis=0,
+            ),
+            axis=0,
+        ),
         preferred_element_type=jnp.float32,
     )
     q_width = HEADS * HEAD_DIM

time: 204 us -> 269 us (1.32)
  the two profiles are of different devices: /device:TPU:0 before, /device:TPU:25 now
where the time goes in v1:
time: 269 us; the launch traced here: 268 us
  waiting for transfers between devices  197 us (73%)
  starting transfers between devices  27.6 us (10%)
  between operations  14.2 us (5%)
  local copies, waits for them, and re-layouts  11.2 us (4%)
  matrix products  9.41 us (3%)
  other arithmetic  7.37 us (3%)
    all_to_all x1, waiting for transfers between devices, body(): lax.all_to_all(jnp.stack([weight_in] * lax.axis_size('ctx')), axis_name='...  169 us
    ppermute x4, waiting for transfers between devices, passed_along(): lax.ppermute(value, axis, [(source, source + steps) for source in range(i...  25.8 us
    ppermute x4, starting transfers between devices, passed_along(): lax.ppermute(value, axis, [(source, source + steps) for source in range(i...  12.2 us
    ppermute x1, starting transfers between devices, passed_along_2(): return lax.ppermute(value, axis, pairs)  8.79 us
    all_to_all x1, starting transfers between devices, body(): lax.all_to_all(jnp.stack([weight_in] * lax.axis_size('ctx')), axis_name='...  6.57 us
    unnamed x12, local copies, waits for them, and re-layouts  6.23 us
  transfers between devices with their start and end apart: 7, of which 5 were waited for; matrix products, arithmetic and copies ran while one was open for 7% of the time, Pallas kernels for 0%

profile of v1, /device:TPU:25, one launch (start us, length us, event | category | flops | bytes accessed | tf_op | source)
XLA Modules:
  0.0 268.1 jit_solution(8056707321220708251)
XLA Ops:
  6.5 4.3 %stack.3 = bf16[16,128,1536]{2,1,0:T(8,128)(2,1)} broadcast(bf16[128,1536]{1,0:T(8,128)(2,1)} %bitcast.117), dimensions={1,2} | broadcast | bytes 6684672 | tf_op jit(solution)/shard_map/stack | solution.py:70
  10.8 6.6 %all-to-all-start = ((bf16[16,128,1536]{2,1,0:T(8,128)(2,1)}), bf16[16,128,1536]{2,1,0:T(8,128)(2,1)}, u32[]{:S(2)}, u32[]{:S(2)}) async-start(bf16[16,128,1536]{2,1,0:T(8,128)(2,1)} %stack.3), calls=%async_computation | async-start | bytes 12582912 | tf_op jit(solution)/shard_map/all_to_all | solution.py:69
  18.9 168.7 %all-to-all-done = bf16[16,128,1536]{2,1,0:T(8,128)(2,1)} async-done(((bf16[16,128,1536]{2,1,0:T(8,128)(2,1)}), bf16[16,128,1536]{2,1,0:T(8,128)(2,1)}, u32[]{:S(2)}, u32[]{:S(2)}) %all-to-all-start) | async-done | bytes 6291488 | tf_op jit(solution)/shard_map/all_to_all | solution.py:69
  187.6 3.8 %fusion.37 = f32[128,1536]{1,0:T(8,128)S(1)} fusion(bf16[2048,1536]{1,0:T(8,128)(2,1)} %bitcast.19, bf16[1,128,2048]{2,1,0:T(8,128)(2,1)S(1)} %copy-done, f32[2048]{0:T(1024)S(1)} %bitcast.124, f32[128]{0:T(128)S(1)} %add_rsqrt_fusion), kind=kOutput, calls=%fused_computation.45 | convolution fusion | flops 806354944 | bytes 7610880 | tf_op jit(solution)/shard_map/dot_general | solution.py:66
  192.3 1.9 collective-permute-start.1
  194.2 8.7 %collective-permute-done.1 = bf16[128,512]{1,0:T(8,128)(2,1)S(1)} collective-permute-done((bf16[128,512]{1,0:T(8,128)(2,1)}, bf16[128,512]{1,0:T(8,128)(2,1)S(1)}, u32[]{:S(2)}, u32[]{:S(2)}) %collective-permute-start.1) | collective-permute-done | bytes 131104 | tf_op jit(solution)/shard_map/ppermute | solution.py:17
  203.0 7.7 %collective-permute-start.2 = (bf16[256,512]{1,0:T(8,128)(2,1)S(1)}, bf16[256,512]{1,0:T(8,128)(2,1)S(1)}, u32[]{:S(2)}, u32[]{:S(2)}) collective-permute-start(bf16[256,512]{1,0:T(8,128)(2,1)S(1)} %maximum_maximum_fusion.1), channel_id=1, source_target_pairs={{0,2},{1,3},{2,4},{3,5},{4,6},{5,7},{6,8},{7,9},{8,10},{9,11},{10,... | collective-permute-start | bytes 786440 | tf_op jit(solution)/shard_map/ppermute | solution.py:17
  211.4 2.5 collective-permute-done.2
  214.0 0.8 maximum_maximum_fusion
  214.8 1.3 collective-permute-start.3
  216.9 1.3 collective-permute-start
  218.5 14.6 %collective-permute-done = bf16[128,512]{1,0:T(8,128)(2,1)} collective-permute-done((bf16[128,512]{1,0:T(8,128)(2,1)}, bf16[128,512]{1,0:T(8,128)(2,1)}, u32[]{:S(2)}, u32[]{:S(2)}) %collective-permute-start) | collective-permute-done | bytes 131104 | tf_op jit(solution)/shard_map/ppermute | solution.py:17
  233.1 1.5 constant_dynamic-update-slice_fusion.4
  237.5 1.7 copy.29
  239.3 6.7 %while.20 = (s32[]{:T(128)}, f32[4,4,128]{2,1,0:T(4,128)S(1)}, f32[4,4,128]{2,1,0:T(4,128)S(1)}, f32[4,4,128,64]{2,3,1,0:T(8,128)S(1)}, s32[128]{0:T(128)S(1)}, ...) while((s32[]{:T(128)}, f32[4,4,128]{2,1,0:T(4,128)S(1)}, ...), condition=%wide.region_13.14_spmd.clone, body=%wide.region_6.13_spmd.clone.sunk | while | flops 282668160 | bytes 15872853 | solution.py:153
  239.4 1.0 fusion.55
  241.3 1.0 fusion.55
  242.9 3.1 %conditional.5 = ((f32[4,4,128]{2,1,0:T(4,128)S(1)}, f32[4,4,128]{2,1,0:T(4,128)S(1)}, f32[4,4,128,64]{2,3,1,0:T(8,128)S(1)})) conditional(s32[]{:T(128)} %convert_element_type.128, (f32[4,4,128]{2,1,0:T(4,128)S(1)}, f32[4,4,128]{2,1,0:T(4,128)S(1)}, f32[4,4,128,64]{2,3,1,0:T(8,128)S(1)}) %tuple.82, (pred[128,512]{0,1:T(8,128)(4,1)S(1)}, s32[]{:T(128)}, ...), branch_computations={%region_9.9_spmd, %region_10.12_spmd} | conditional | flops 282333184 | bytes 15794262 | solution.py:125
  243.8 1.0 fusion.4
  244.8 1.2 fusion.8
  246.0 1.1 conditional.2
  247.2 2.9 %fusion.29 = bf16[128,2048]{1,0:T(8,128)(2,1)S(1)} fusion(bf16[128,1024]{0,1:T(8,128)(2,1)S(1)} %bitcast.106, bf16[1,1024,2048]{2,1,0:T(8,128)(2,1)} %all-gather.3.cloned.1.call-done, bf16[1,128,2048]{2,1,0:T(8,128)(2,1)S(1)} %copy-done), kind=kOutput, calls=%fused_computation.37 | convolution fusion | flops 537657344 | bytes 5505024 | tf_op jit(solution)/shard_map/dot_general | solution.py:165
  250.2 8.8 %collective-permute-start.4 = (bf16[128,2048]{1,0:T(8,128)(2,1)S(1)}, bf16[128,2048]{1,0:T(8,128)(2,1)S(1)}, u32[]{:S(2)}, u32[]{:S(2)}) collective-permute-start(bf16[128,2048]{1,0:T(8,128)(2,1)S(1)} %fusion.29), channel_id=1, source_target_pairs={{0,16},{16,0},{1,17},{17,1},{2,18},{18,2},{3,19},{19,3},{4,20},{20... | collective-permute-start | bytes 1572872 | tf_op jit(solution)/shard_map/ppermute | solution.py:23
  259.0 1.5 collective-permute-done.4
  (66 shorter events, 9.5 us)
Async XLA Ops:
  10.8 7.3 %copy-start.2 = (s32[2,4]{1,0:T(2,128)S(1)}, s32[2,4]{1,0:T(2,128)}, u32[]{:S(2)}) copy-start(s32[2,4]{1,0:T(2,128)} %param.15) | copy-start | bytes 100
  10.8 7.7 %copy-start = (bf16[1,128,2048]{2,1,0:T(8,128)(2,1)S(1)}, bf16[1,128,2048]{2,1,0:T(8,128)(2,1)}, u32[]{:S(2)}) copy-start(bf16[1,128,2048]{2,1,0:T(8,128)(2,1)} %param.11) | copy-start | bytes 1572868
  10.8 176.8 %copy-start.1 = (f32[1,2048]{1,0:T(1,128)S(1)}, f32[1,2048]{1,0:T(1,128)}, u32[]{:S(2)}) copy-start(f32[1,2048]{1,0:T(1,128)} %param.12) | copy-start | bytes 24580
  10.8 176.8 %all-to-all-start = ((bf16[16,128,1536]{2,1,0:T(8,128)(2,1)}), bf16[16,128,1536]{2,1,0:T(8,128)(2,1)}, u32[]{:S(2)}, u32[]{:S(2)}) async-start(bf16[16,128,1536]{2,1,0:T(8,128)(2,1)} %stack.3), calls=%async_computation | async-start | bytes 12582912 | tf_op jit(solution)/shard_map/all_to_all | solution.py:69
  17.4 229.8 %all-gather.3.cloned.1.call-start = ((), (), s32[]{:S(2)}) async-start(), calls=%async_computation.1 | async-start | bytes 4456448 | tf_op jit(solution)/shard_map/all_gather | solution.py:167
  192.3 10.6 %collective-permute-start.1 = (bf16[128,512]{1,0:T(8,128)(2,1)}, bf16[128,512]{1,0:T(8,128)(2,1)S(1)}, u32[]{:S(2)}, u32[]{:S(2)}) collective-permute-start(bf16[128,512]{1,0:T(8,128)(2,1)} %pad_maximum_fusion.1), channel_id=1, source_target_pairs={{0,1},{1,2},{2,3},{3,4},{4,5},{5,6},{6,7},{7,8},{8,9},{9,10},{10,1... | collective-permute-start | bytes 393224 | tf_op jit(solution)/shard_map/ppermute | solution.py:17
  203.0 11.0 %collective-permute-start.2 = (bf16[256,512]{1,0:T(8,128)(2,1)S(1)}, bf16[256,512]{1,0:T(8,128)(2,1)S(1)}, u32[]{:S(2)}, u32[]{:S(2)}) collective-permute-start(bf16[256,512]{1,0:T(8,128)(2,1)S(1)} %maximum_maximum_fusion.1), channel_id=1, source_target_pairs={{0,2},{1,3},{2,4},{3,5},{4,6},{5,7},{6,8},{7,9},{8,10},{9,11},{10,... | collective-permute-start | bytes 786440 | tf_op jit(solution)/shard_map/ppermute | solution.py:17
  214.8 19.9 %collective-permute-start.3 = (bf16[512,512]{1,0:T(8,128)(2,1)}, bf16[512,512]{1,0:T(8,128)(2,1)S(1)}, u32[]{:S(2)}, u32[]{:S(2)}) collective-permute-start(bf16[512,512]{1,0:T(8,128)(2,1)} %maximum_maximum_fusion), channel_id=1, source_target_pairs={{0,4},{1,5},{2,6},{3,7},{4,8},{5,9},{6,10},{7,11},{8,12},{9,13},{1... | collective-permute-start | bytes 1572872 | tf_op jit(solution)/shard_map/ppermute | solution.py:17
  216.9 16.3 %collective-permute-start = (bf16[128,512]{1,0:T(8,128)(2,1)}, bf16[128,512]{1,0:T(8,128)(2,1)}, u32[]{:S(2)}, u32[]{:S(2)}) collective-permute-start(bf16[128,512]{1,0:T(8,128)(2,1)} %pad_maximum_fusion.1), channel_id=1, source_target_pairs={{0,8},{1,9},{2,10},{3,11},{4,12},{5,13},{6,14},{7,15},{16,24},{17,... | collective-permute-start | bytes 393224 | tf_op jit(solution)/shard_map/ppermute | solution.py:17
  250.2 10.3 %collective-permute-start.4 = (bf16[128,2048]{1,0:T(8,128)(2,1)S(1)}, bf16[128,2048]{1,0:T(8,128)(2,1)S(1)}, u32[]{:S(2)}, u32[]{:S(2)}) collective-permute-start(bf16[128,2048]{1,0:T(8,128)(2,1)S(1)} %fusion.29), channel_id=1, source_target_pairs={{0,16},{16,0},{1,17},{17,1},{2,18},{18,2},{3,19},{19,3},{4,20},{20... | collective-permute-start | bytes 1572872 | tf_op jit(solution)/shard_map/ppermute | solution.py:23
Sparse Core Ops, SparseCore 0:
  20.9 164.6 all-gather.2
